TPU v7x, 32 devices: a whole 2x2x4 slice. The times are simulated.
32 devices in a mesh: dp: 2 (over core), row: 4 (over y, x), col: 4 (over z).
Axes of the slice: x: 2, y: 2, z: 4, core: 2. Of those that a mesh axis runs over, the one named last changes fastest.
Arguments:
- block_input: bfloat16 [8192, 2048], P(('dp', 'row')), may hold values from -6 to 6
- segment_ids: int32 [8192], P(('dp', 'row')), may hold values from 0 to 3, as said below
- positions: int32 [8192], P(('dp', 'row')), may hold values from 0 to 1023, as said below
- w_query: bfloat16 [2048, 2048], P('row', 'col'), as said below
- w_key: bfloat16 [2048, 2048], P('row', 'col'), as said below
- w_value: bfloat16 [2048, 2048], P('row', 'col'), may hold values from -0.125 to 0.125
- w_out: bfloat16 [2048, 2048], P('col', 'row'), may hold values from -0.125 to 0.125
- w_gate: bfloat16 [2048, 8192], P('row', 'col'), may hold values from -0.125 to 0.125
- w_up: bfloat16 [2048, 8192], P('row', 'col'), may hold values from -0.125 to 0.125
- w_down: bfloat16 [8192, 2048], P('col', 'row'), may hold values from -0.0625 to 0.0625
- query_gain: float32 [2048], P('col'), may hold values from 0.25 to 1.75
- key_gain: float32 [2048], P('col'), may hold values from 0.25 to 1.75
- attn_gain: float32 [2048], replicated, may hold values from 0.25 to 1.75
- mlp_gain: float32 [2048], replicated, may hold values from 0.25 to 1.75
- grad_output: bfloat16 [8192, 2048], P(('dp', 'row')), as said below
Outputs:
- block_output: bfloat16 [8192, 2048], P(('dp', 'row'))
- grad_input: float32 [8192, 2048], P(('dp', 'row'))
- grad_w_query: float32 [2048, 2048], P('row', 'col')
- grad_w_key: float32 [2048, 2048], P('row', 'col')
- grad_w_value: float32 [2048, 2048], P('row', 'col')
- grad_w_out: float32 [2048, 2048], P('col', 'row')
- grad_w_gate: float32 [2048, 8192], P('row', 'col')
- grad_w_up: float32 [2048, 8192], P('row', 'col')
- grad_w_down: float32 [8192, 2048], P('col', 'row')
- grad_query_gain: float32 [2048], P('col')
- grad_key_gain: float32 [2048], P('col')
- grad_attn_gain: float32 [2048], replicated
- grad_mlp_gain: float32 [2048], replicated
Inputs may be any that keep to these rules, and one draw needn't show every extreme that they name: `segment_ids`: within each sequence of 1024 tokens the ids never fall. `positions`: the index of a token counted from the first token with the same id in its sequence. `w_query`: scaled to the fan-in 2048. `w_key`: scaled to the fan-in 2048. `grad_output`: of order one in every row.
All inputs are finite; a program needn't handle non-finite values.
Results may differ from a plain program's by a relative error of at most 0.02.
Values may be sent and summed in bfloat16 or wider, within the bound.
No kernel may reach another device: no remote copies, remote signals or barrier semaphores. Data moves between devices by JAX's collectives and lax.ppermute only.
A program may use at most 320 MiB of HBM per device.

v0:
```python
import jax
import jax.numpy as jnp
from jax import lax
from jax.sharding import PartitionSpec as P

HD = 128
LEN = 1024
EPS = 1e-06
THETA = 500000.0
NEG_FILL = -1e30


def plain_dot(left_mat, right_mat):
    return jnp.dot(left_mat, right_mat, preferred_element_type=jnp.float32)


def times_transposed(left_mat, right_mat):
    return lax.dot_general(
        left_mat, right_mat, (((1,), (1,)), ((), ())), preferred_element_type=jnp.float32
    )


def left_transposed(left_mat, right_mat):
    return lax.dot_general(
        left_mat, right_mat, (((0,), (0,)), ((), ())), preferred_element_type=jnp.float32
    )


def rope_tables(positions):
    half_dim = HD // 2
    inv_freq = THETA ** (-(jnp.arange(half_dim, dtype=jnp.float32) * 2.0) / HD)
    angles = positions.astype(jnp.float32)[:, None] * inv_freq[None, :]
    cosine = jnp.concatenate([jnp.cos(angles), jnp.cos(angles)], axis=-1)
    sine_tab = jnp.concatenate([jnp.sin(angles), jnp.sin(angles)], axis=-1)
    return (cosine, sine_tab)


def rotate(values):
    first_half = values[..., : HD // 2]
    second_half = values[..., HD // 2 :]
    return jnp.concatenate([-second_half, first_half], axis=-1)


def rotate_back(values):
    first_half = values[..., : HD // 2]
    second_half = values[..., HD // 2 :]
    return jnp.concatenate([second_half, -first_half], axis=-1)


def block_mask(seg_seq, first_row, block_rows):
    length = seg_seq.shape[0]
    query_index = first_row + jnp.arange(block_rows)
    key_index = jnp.arange(length)
    query_seg = seg_seq[first_row : first_row + block_rows]
    return (
        (query_seg[:, None] == seg_seq[None, :]) & (key_index[None, :] <= query_index[:, None])
    )[None]


def attend_forward(packed):
    query_rot, key_rot, value_heads, seg_seq = packed
    length = query_rot.shape[0]
    block_rows = min(512, length)
    score_scale = HD ** (-0.5)
    output_list = []
    log_list = []
    for first_row in range(0, length, block_rows):
        query_blk = query_rot[first_row : first_row + block_rows]
        scores = (
            jnp.einsum("qhd,khd->hqk", query_blk, key_rot, preferred_element_type=jnp.float32)
            * score_scale
        )
        allowed = block_mask(seg_seq, first_row, block_rows)
        masked = jnp.where(allowed, scores, NEG_FILL)
        row_peak = jnp.max(masked, axis=-1, keepdims=True)
        row_total = jnp.sum(jnp.exp(masked - row_peak), axis=-1, keepdims=True)
        log_total = row_peak + jnp.log(row_total)
        probs_b = jnp.where(allowed, jnp.exp(scores - log_total), 0.0).astype(jnp.bfloat16)
        attended = jnp.einsum(
            "hqk,khd->qhd", probs_b, value_heads, preferred_element_type=jnp.float32
        ).astype(jnp.bfloat16)
        output_list.append(attended)
        log_list.append(log_total[..., 0])
    return (jnp.concatenate(output_list, axis=0), jnp.concatenate(log_list, axis=1))


def attend_backward(packed):
    query_rot, key_rot, value_heads, seg_seq, attended, log_total, grad_att = packed
    length = query_rot.shape[0]
    block_rows = min(512, length)
    score_scale = HD ** (-0.5)
    delta = jnp.sum(grad_att.astype(jnp.float32) * attended.astype(jnp.float32), axis=-1)
    grad_key = jnp.zeros(key_rot.shape, jnp.float32)
    grad_value = jnp.zeros(value_heads.shape, jnp.float32)
    grad_query_list = []
    for first_row in range(0, length, block_rows):
        query_blk = query_rot[first_row : first_row + block_rows]
        grad_blk = grad_att[first_row : first_row + block_rows]
        scores = (
            jnp.einsum("qhd,khd->hqk", query_blk, key_rot, preferred_element_type=jnp.float32)
            * score_scale
        )
        allowed = block_mask(seg_seq, first_row, block_rows)
        probs = jnp.where(
            allowed, jnp.exp(scores - log_total[:, first_row : first_row + block_rows, None]), 0.0
        )
        probs_b = probs.astype(jnp.bfloat16)
        grad_probs = jnp.einsum(
            "qhd,khd->hqk", grad_blk, value_heads, preferred_element_type=jnp.float32
        )
        delta_blk = jnp.transpose(delta[first_row : first_row + block_rows])[:, :, None]
        grad_scores = (probs * (grad_probs - delta_blk) * score_scale).astype(jnp.bfloat16)
        grad_query_list.append(
            jnp.einsum("hqk,khd->qhd", grad_scores, key_rot, preferred_element_type=jnp.float32)
        )
        grad_key = grad_key + jnp.einsum(
            "hqk,qhd->khd", grad_scores, query_blk, preferred_element_type=jnp.float32
        )
        grad_value = grad_value + jnp.einsum(
            "hqk,qhd->khd", probs_b, grad_blk, preferred_element_type=jnp.float32
        )
    return (jnp.concatenate(grad_query_list, axis=0), grad_key, grad_value)


def shards(
    block_input,
    segment_ids,
    positions,
    w_query,
    w_key,
    w_value,
    w_out,
    w_gate,
    w_up,
    w_down,
    query_gain,
    key_gain,
    attn_gain,
    mlp_gain,
    grad_output,
):
    tokens_here = block_input.shape[0]
    seq_count = tokens_here // LEN
    width = block_input.shape[1]
    local_width = w_query.shape[1]
    local_heads = local_width // HD
    gathered = (
        lax.all_gather(w_query, "row", axis=0, tiled=True),
        lax.all_gather(w_key, "row", axis=0, tiled=True),
        lax.all_gather(w_value, "row", axis=0, tiled=True),
        lax.all_gather(w_out, "row", axis=1, tiled=True),
        lax.all_gather(w_gate, "row", axis=0, tiled=True),
        lax.all_gather(w_up, "row", axis=0, tiled=True),
        lax.all_gather(w_down, "row", axis=1, tiled=True),
    )
    full_query, full_key, full_value, full_out, full_gate, full_up, full_down = gathered
    query_raw = plain_dot(block_input, full_query)
    key_raw = plain_dot(block_input, full_key)
    value_raw = plain_dot(block_input, full_value)
    query_sq, key_sq = lax.psum(
        (jnp.sum(query_raw * query_raw, axis=1), jnp.sum(key_raw * key_raw, axis=1)), "col"
    )
    query_scale = lax.rsqrt(query_sq / width + EPS)[:, None]
    key_scale = lax.rsqrt(key_sq / width + EPS)[:, None]
    query_unit = query_raw * query_scale
    key_unit = key_raw * key_scale
    cosine, sine_tab = rope_tables(positions)

    def turn(values):
        head_view = values.reshape(tokens_here, local_heads, HD)
        return head_view * cosine[:, None, :] + rotate(head_view) * sine_tab[:, None, :]

    def unturn(values):
        back = values * cosine[:, None, :] + rotate_back(values * sine_tab[:, None, :])
        return back.reshape(tokens_here, local_width)

    seq_shape = (seq_count, LEN, local_heads, HD)
    query_rot = turn(query_unit * query_gain).astype(jnp.bfloat16).reshape(seq_shape)
    key_rot = turn(key_unit * key_gain).astype(jnp.bfloat16).reshape(seq_shape)
    value_heads = value_raw.astype(jnp.bfloat16).reshape(seq_shape)
    seg_view = segment_ids.reshape(seq_count, LEN)
    attended, log_total = lax.map(attend_forward, (query_rot, key_rot, value_heads, seg_view))
    attended_flat = attended.reshape(tokens_here, local_width)
    attn_raw = lax.psum(plain_dot(attended_flat, full_out), "col")
    attn_scale = lax.rsqrt(jnp.mean(attn_raw * attn_raw, axis=1, keepdims=True) + EPS)
    attn_unit = attn_raw * attn_scale
    hidden = block_input.astype(jnp.float32) + attn_unit * attn_gain
    hidden_b = hidden.astype(jnp.bfloat16)
    gate_proj = plain_dot(hidden_b, full_gate)
    up_proj = plain_dot(hidden_b, full_up)
    gate_sig = jax.nn.sigmoid(gate_proj)
    gate_act = gate_proj * gate_sig
    mixed_act = (gate_act * up_proj).astype(jnp.bfloat16)
    down_raw = lax.psum(plain_dot(mixed_act, full_down), "col")
    down_scale = lax.rsqrt(jnp.mean(down_raw * down_raw, axis=1, keepdims=True) + EPS)
    down_unit = down_raw * down_scale
    block_output = (hidden + down_unit * mlp_gain).astype(jnp.bfloat16)
    regathered = (
        lax.all_gather(w_query, "row", axis=0, tiled=True),
        lax.all_gather(w_key, "row", axis=0, tiled=True),
        lax.all_gather(w_value, "row", axis=0, tiled=True),
        lax.all_gather(w_out, "row", axis=1, tiled=True),
        lax.all_gather(w_gate, "row", axis=0, tiled=True),
        lax.all_gather(w_up, "row", axis=0, tiled=True),
        lax.all_gather(w_down, "row", axis=1, tiled=True),
    )
    full_query, full_key, full_value, full_out, full_gate, full_up, full_down = regathered
    grad_y = grad_output.astype(jnp.float32)
    grad_mlp_gain = jnp.sum(grad_y * down_unit, axis=0)
    down_dz = grad_y * mlp_gain
    grad_down_in = (
        down_scale * (down_dz - down_unit * jnp.mean(down_dz * down_unit, axis=1, keepdims=True))
    ).astype(jnp.bfloat16)
    grad_w_down = left_transposed(mixed_act, grad_down_in)
    grad_mixed = times_transposed(grad_down_in, full_down)
    grad_gate_in = (grad_mixed * up_proj * gate_sig * (1.0 + gate_proj * (1.0 - gate_sig))).astype(
        jnp.bfloat16
    )
    grad_up_in = (grad_mixed * gate_act).astype(jnp.bfloat16)
    grad_w_gate = left_transposed(hidden_b, grad_gate_in)
    grad_w_up = left_transposed(hidden_b, grad_up_in)
    mlp_part = times_transposed(grad_gate_in, full_gate) + times_transposed(grad_up_in, full_up)
    grad_hidden = grad_y + lax.psum(mlp_part, "col")
    grad_attn_gain = jnp.sum(grad_hidden * attn_unit, axis=0)
    attn_dz = grad_hidden * attn_gain
    grad_attn_in = (
        attn_scale * (attn_dz - attn_unit * jnp.mean(attn_dz * attn_unit, axis=1, keepdims=True))
    ).astype(jnp.bfloat16)
    grad_w_out = left_transposed(attended_flat, grad_attn_in)
    grad_att = times_transposed(grad_attn_in, full_out).astype(jnp.bfloat16).reshape(seq_shape)
    grad_query_rot, grad_key_rot, grad_value_heads = lax.map(
        attend_backward, (query_rot, key_rot, value_heads, seg_view, attended, log_total, grad_att)
    )
    head_shape = (tokens_here, local_heads, HD)
    grad_query_norm = unturn(grad_query_rot.reshape(head_shape))
    grad_key_norm = unturn(grad_key_rot.reshape(head_shape))
    grad_query_gain = jnp.sum(grad_query_norm * query_unit, axis=0)
    grad_key_gain = jnp.sum(grad_key_norm * key_unit, axis=0)
    query_dz = grad_query_norm * query_gain
    key_dz = grad_key_norm * key_gain
    query_dot, key_dot = lax.psum(
        (jnp.sum(query_dz * query_unit, axis=1), jnp.sum(key_dz * key_unit, axis=1)), "col"
    )
    grad_query_in = (query_scale * (query_dz - query_unit * (query_dot / width)[:, None])).astype(
        jnp.bfloat16
    )
    grad_key_in = (key_scale * (key_dz - key_unit * (key_dot / width)[:, None])).astype(
        jnp.bfloat16
    )
    grad_value_in = grad_value_heads.reshape(tokens_here, local_width).astype(jnp.bfloat16)
    input_part = (
        times_transposed(grad_query_in, full_query)
        + times_transposed(grad_key_in, full_key)
        + times_transposed(grad_value_in, full_value)
    )
    grad_input = grad_hidden + lax.psum(input_part.astype(jnp.bfloat16), "col").astype(jnp.float32)
    grad_w_query = left_transposed(block_input, grad_query_in)
    grad_w_key = left_transposed(block_input, grad_key_in)
    grad_w_value = left_transposed(block_input, grad_value_in)
    row_grads = (
        lax.psum_scatter(
            grad_w_query.astype(jnp.bfloat16), "row", scatter_dimension=0, tiled=True
        ).astype(jnp.float32),
        lax.psum_scatter(
            grad_w_key.astype(jnp.bfloat16), "row", scatter_dimension=0, tiled=True
        ).astype(jnp.float32),
        lax.psum_scatter(
            grad_w_value.astype(jnp.bfloat16), "row", scatter_dimension=0, tiled=True
        ).astype(jnp.float32),
        lax.psum_scatter(
            grad_w_out.astype(jnp.bfloat16), "row", scatter_dimension=1, tiled=True
        ).astype(jnp.float32),
        lax.psum_scatter(
            grad_w_gate.astype(jnp.bfloat16), "row", scatter_dimension=0, tiled=True
        ).astype(jnp.float32),
        lax.psum_scatter(
            grad_w_up.astype(jnp.bfloat16), "row", scatter_dimension=0, tiled=True
        ).astype(jnp.float32),
        lax.psum_scatter(
            grad_w_down.astype(jnp.bfloat16), "row", scatter_dimension=1, tiled=True
        ).astype(jnp.float32),
    )
    data_grads = (
        lax.psum(row_grads[0].astype(jnp.bfloat16), "dp").astype(jnp.float32),
        lax.psum(row_grads[1].astype(jnp.bfloat16), "dp").astype(jnp.float32),
        lax.psum(row_grads[2].astype(jnp.bfloat16), "dp").astype(jnp.float32),
        lax.psum(row_grads[3].astype(jnp.bfloat16), "dp").astype(jnp.float32),
        lax.psum(row_grads[4].astype(jnp.bfloat16), "dp").astype(jnp.float32),
        lax.psum(row_grads[5].astype(jnp.bfloat16), "dp").astype(jnp.float32),
        lax.psum(row_grads[6].astype(jnp.bfloat16), "dp").astype(jnp.float32),
    )
    gain_grads = lax.psum(
        (grad_query_gain, grad_key_gain, grad_attn_gain, grad_mlp_gain), ("dp", "row")
    )
    return (
        block_output,
        grad_input,
        data_grads[0],
        data_grads[1],
        data_grads[2],
        data_grads[3],
        data_grads[4],
        data_grads[5],
        data_grads[6],
        gain_grads[0],
        gain_grads[1],
        gain_grads[2],
        gain_grads[3],
    )


def solution(mesh):
    in_specs = (
        P(("dp", "row"), None),
        P(("dp", "row")),
        P(("dp", "row")),
        P("row", "col"),
        P("row", "col"),
        P("row", "col"),
        P("col", "row"),
        P("row", "col"),
        P("row", "col"),
        P("col", "row"),
        P("col"),
        P("col"),
        P(),
        P(),
        P(("dp", "row"), None),
    )
    out_specs = (
        P(("dp", "row"), None),
        P(("dp", "row"), None),
        P("row", "col"),
        P("row", "col"),
        P("row", "col"),
        P("col", "row"),
        P("row", "col"),
        P("row", "col"),
        P("col", "row"),
        P("col"),
        P("col"),
        P(),
        P(),
    )
    return jax.shard_map(shards, mesh=mesh, in_specs=in_specs, out_specs=out_specs, check_vma=False)
```

profile of v0, /device:TPU:0, one launch (start us, length us, event | category | flops | bytes accessed | tf_op | source)
XLA Modules:
  0.0 2085.5 jit_solution(18045758009475935675)
XLA Ops:
  15.1 32.7 %all-gather.12.cloned.1.call-done = bf16[2048,512]{1,0:T(8,128)(2,1)} async-done(((bf16[512,512]{1,0:T(8,128)(2,1)}), bf16[2048,512]{1,0:T(8,128)(2,1)}) %all-gather.12.cloned.1.call-update) | async-done | bytes 2097168 | tf_op jit(solution)/shard_map/all_gather | solution.py:149
  54.4 30.5 %all-gather.10.cloned.1.call-done = bf16[2048,512]{1,0:T(8,128)(2,1)} async-done(((bf16[512,512]{1,0:T(8,128)(2,1)}), bf16[2048,512]{1,0:T(8,128)(2,1)}) %all-gather.10.cloned.1.call-update) | async-done | bytes 2097168 | tf_op jit(solution)/shard_map/all_gather | solution.py:148
  141.4 17.3 all-gather.14.cloned.1.call-done
  168.0 288.8 %all-reduce.10.cloned.1.call-done = f32[1024,2048]{1,0:T(8,128)} async-done(((f32[1024,2048]{1,0:T(8,128)}), f32[1024,2048]{1,0:T(8,128)}) %all-reduce.10.cloned.1.call-update) | async-done | bytes 8388624 | tf_op jit(solution)/shard_map/psum | solution.py:184
  467.6 77.5 %all-gather.16.cloned.1.call-done = bf16[2048,2048]{1,0:T(8,128)(2,1)} async-done(((bf16[512,2048]{1,0:T(8,128)(2,1)}), bf16[2048,2048]{1,0:T(8,128)(2,1)}) %all-gather.16.cloned.1.call-update) | async-done | bytes 8388624 | tf_op jit(solution)/shard_map/all_gather | solution.py:152
  545.1 14.5 fusion.42
  559.6 74.8 %all-gather.18.cloned.1.call-done = bf16[2048,2048]{1,0:T(8,128)(2,1)} async-done(((bf16[512,2048]{1,0:T(8,128)(2,1)}), bf16[2048,2048]{1,0:T(8,128)(2,1)}) %all-gather.18.cloned.1.call-update) | async-done | bytes 8388624 | tf_op jit(solution)/shard_map/all_gather | solution.py:153
  634.4 17.0 multiply_convert_fusion.5
  651.4 72.3 %all-gather.20.cloned.1.call-done = bf16[2048,2048]{1,0:T(8,128)(2,1)} async-done(((bf16[2048,512]{1,0:T(8,128)(2,1)}), bf16[2048,2048]{1,0:T(8,128)(2,1)}) %all-gather.20.cloned.1.call-update) | async-done | bytes 8388624 | tf_op jit(solution)/shard_map/all_gather | solution.py:154
  723.6 14.5 fusion.43
  738.2 290.9 %all-reduce.12.cloned.1.call-done = f32[1024,2048]{1,0:T(8,128)} async-done(((f32[1024,2048]{1,0:T(8,128)}), f32[1024,2048]{1,0:T(8,128)}) %all-reduce.12.cloned.1.call-update) | async-done | bytes 8388624 | tf_op jit(solution)/shard_map/psum | solution.py:194
  1042.5 19.7 multiply_convert_fusion.3
  1074.9 13.6 convolution_add_fusion
  1090.6 287.9 %all-reduce.14.cloned.1.call-done = f32[1024,2048]{1,0:T(8,128)} async-done(((f32[1024,2048]{1,0:T(8,128)}), f32[1024,2048]{1,0:T(8,128)}) %all-reduce.14.cloned.1.call-update) | async-done | bytes 8388624 | tf_op jit(solution)/shard_map/psum | solution.py:223
  1499.6 14.4 convolution_convert_fusion
  1514.1 14.1 convolution_convert_fusion.2
  1528.3 14.7 convolution_convert_fusion.1
  1558.5 38.0 %reduce-scatter.8.cloned.1.call-done = bf16[512,512]{0,1:T(8,128)(2,1)} async-done(((bf16[2048,512]{0,1:T(8,128)(2,1)}), bf16[512,512]{0,1:T(8,128)(2,1)}) %reduce-scatter.8.cloned.1.call-update) | async-done | bytes 524304 | tf_op jit(solution)/shard_map/reduce_scatter | solution.py:261
  1596.5 89.3 %reduce-scatter.20.cloned.1.call-done = bf16[2048,512]{1,0:T(8,128)(2,1)} async-done(((bf16[2048,2048]{1,0:T(8,128)(2,1)}), bf16[2048,512]{1,0:T(8,128)(2,1)}) %reduce-scatter.20.cloned.1.call-update) | async-done | bytes 2097168 | tf_op jit(solution)/shard_map/reduce_scatter | solution.py:279
  1685.8 89.8 %reduce-scatter.16.cloned.1.call-done = bf16[512,2048]{1,0:T(8,128)(2,1)} async-done(((bf16[2048,2048]{1,0:T(8,128)(2,1)}), bf16[512,2048]{1,0:T(8,128)(2,1)}) %reduce-scatter.16.cloned.1.call-update) | async-done | bytes 2097168 | tf_op jit(solution)/shard_map/reduce_scatter | solution.py:273
  1775.6 89.3 %reduce-scatter.18.cloned.1.call-done = bf16[512,2048]{1,0:T(8,128)(2,1)} async-done(((bf16[2048,2048]{1,0:T(8,128)(2,1)}), bf16[512,2048]{1,0:T(8,128)(2,1)}) %reduce-scatter.18.cloned.1.call-update) | async-done | bytes 2097168 | tf_op jit(solution)/shard_map/reduce_scatter | solution.py:276
  1865.6 27.9 %all-reduce = (f32[512]{0:T(512)}, f32[512]{0:T(512)}, f32[2048]{0:T(1024)}, f32[2048]{0:T(1024)}) all-reduce(f32[512]{0:T(512)S(1)} %get-tuple-element.86, f32[512]{0:T(512)S(1)} %get-tuple-element.84, f32[2048]{0:T(1024)S(1)} %copy-done.64, f32[2048]{0:T(1024)S(1)} %copy-done.65), channel_id=1, replica_groups=mesh['dp'=2,'row'=4,'col'=4] {'dp','row'}, use_global_device_ids=true, to_apply=%region_36.37 | all-reduce | flops 5120 | bytes 40960 | tf_op jit(solution)/shard_map/psum | solution.py:292
  1893.5 129.3 %all-reduce.16.cloned.1.call-done = bf16[1024,2048]{1,0:T(8,128)(2,1)} async-done(((bf16[1024,2048]{1,0:T(8,128)(2,1)}), bf16[1024,2048]{1,0:T(8,128)(2,1)}) %all-reduce.16.cloned.1.call-update) | async-done | bytes 4194320 | tf_op jit(solution)/shard_map/psum | solution.py:256
  2034.7 29.7 %all-reduce.18.cloned.1.call-done = (bf16[512,512]{0,1:T(8,128)(2,1)}, bf16[512,512]{0,1:T(8,128)(2,1)}, bf16[512,512]{0,1:T(8,128)(2,1)}, bf16[512,512]{1,0:T(8...) async-done(((bf16[512,512]{0,1:T(8,128)(2,1)}, bf16[512,512]{0,1:T(8,128)(2,1)}, bf16[512,512]{0,1:T(8,128)(2,1)}, ...) | async-done | bytes 8388624 | tf_op jit(solution)/shard_map/psum | solution.py:284
  (291 shorter events, 281.6 us)
Async XLA Ops:
  7.2 40.6 %all-gather.12.cloned.1.call-start = ((), (), s32[]{:S(2)}) async-start(), calls=%async_computation.9 | async-start | bytes 2621440 | tf_op jit(solution)/shard_map/all_gather | solution.py:149
  7.9 76.9 %all-gather.10.cloned.1.call-start = ((), (), s32[]{:S(2)}) async-start(), calls=%async_computation.8 | async-start | bytes 2621440 | tf_op jit(solution)/shard_map/all_gather | solution.py:148
  8.7 119.8 %all-gather.8.cloned.1.call-start = ((), (), s32[]{:S(2)}) async-start(), calls=%async_computation.7 | async-start | bytes 2621440 | tf_op jit(solution)/shard_map/all_gather | solution.py:150
  9.4 149.2 %all-gather.14.cloned.1.call-start = ((), (), s32[]{:S(2)}) async-start(), calls=%async_computation.10 | async-start | bytes 2621440 | tf_op jit(solution)/shard_map/all_gather | solution.py:151
  10.0 446.9 %all-reduce.10.cloned.1.call-start = ((), (), s32[]{:S(2)}) async-start(), calls=%async_computation.11 | async-start | bytes 16777216 | tf_op jit(solution)/shard_map/psum | solution.py:184
  12.8 103.1 %copy-start.22 = (f32[1024,128]{1,0:T(8,128)}, f32[1024,128]{1,0:T(8,128)S(1)}, u32[]{:S(2)}) copy-start(f32[1024,128]{1,0:T(8,128)S(1)} %pad_maximum_fusion.2) | copy-start | bytes 1572868
  165.9 379.2 %all-gather.16.cloned.1.call-start = ((), (), s32[]{:S(2)}) async-start(), calls=%async_computation.12 | async-start | bytes 10485760 | tf_op jit(solution)/shard_map/all_gather | solution.py:152
  166.5 467.9 %all-gather.18.cloned.1.call-start = ((), (), s32[]{:S(2)}) async-start(), calls=%async_computation.13 | async-start | bytes 10485760 | tf_op jit(solution)/shard_map/all_gather | solution.py:153
  167.2 556.4 %all-gather.20.cloned.1.call-start = ((), (), s32[]{:S(2)}) async-start(), calls=%async_computation.14 | async-start | bytes 10485760 | tf_op jit(solution)/shard_map/all_gather | solution.py:154
  168.0 293.7 %copy-start.56 = (f32[2048]{0:T(1024)S(1)}, f32[2048]{0:T(1024)}, u32[]{:S(2)}) copy-start(f32[2048]{0:T(1024)} %param.27) | copy-start | bytes 24580
  168.0 861.2 %all-reduce.12.cloned.1.call-start = ((), (), s32[]{:S(2)}) async-start(), calls=%async_computation.15 | async-start | bytes 16777216 | tf_op jit(solution)/shard_map/psum | solution.py:194
  738.2 295.1 %copy-start.55 = (f32[2048]{0:T(1024)S(1)}, f32[2048]{0:T(1024)}, u32[]{:S(2)}) copy-start(f32[2048]{0:T(1024)} %param.28) | copy-start | bytes 24580
  738.2 640.3 %all-reduce.14.cloned.1.call-start = ((), (), s32[]{:S(2)}) async-start(), calls=%async_computation.16 | async-start | bytes 16777216 | tf_op jit(solution)/shard_map/psum | solution.py:223
  1088.5 290.0 %copy-start.57 = (f32[2048]{0:T(1024)S(1)}, f32[2048]{0:T(1024)}, u32[]{:S(2)}) copy-start(f32[2048]{0:T(1024)} %param.27) | copy-start | bytes 24580
  1088.5 290.0 %copy-start.63 = (f32[1024]{0:T(1024)S(1)}, f32[1024]{0:T(1024)}, u32[]{:S(2)}) copy-start(f32[1024]{0:T(1024)} %copy-done.62) | copy-start | bytes 12292
  1088.6 466.7 %reduce-scatter.12.cloned.1.call-start = ((), (), s32[]{:S(2)}) async-start(), calls=%async_computation.20 | async-start | bytes 2621440 | tf_op jit(solution)/shard_map/reduce_scatter | solution.py:267
  1433.6 121.6 %reduce-scatter.10.cloned.1.call-start = ((), (), s32[]{:S(2)}) async-start(), calls=%async_computation.19 | async-start | bytes 2621440 | tf_op jit(solution)/shard_map/reduce_scatter | solution.py:264
  1486.4 72.1 %reduce-scatter.14.cloned.1.call-start = ((), (), s32[]{:S(2)}) async-start(), calls=%async_computation.21 | async-start | bytes 2621440 | tf_op jit(solution)/shard_map/reduce_scatter | solution.py:270
  1492.7 103.8 %reduce-scatter.8.cloned.1.call-start = ((), (), s32[]{:S(2)}) async-start(), calls=%async_computation.18 | async-start | bytes 2621440 | tf_op jit(solution)/shard_map/reduce_scatter | solution.py:261
  1499.6 186.2 %reduce-scatter.20.cloned.1.call-start = ((), (), s32[]{:S(2)}) async-start(), calls=%async_computation.24 | async-start | bytes 10485760 | tf_op jit(solution)/shard_map/reduce_scatter | solution.py:279
  1514.1 261.5 %reduce-scatter.16.cloned.1.call-start = ((), (), s32[]{:S(2)}) async-start(), calls=%async_computation.22 | async-start | bytes 10485760 | tf_op jit(solution)/shard_map/reduce_scatter | solution.py:273
  1528.2 336.7 %reduce-scatter.18.cloned.1.call-start = ((), (), s32[]{:S(2)}) async-start(), calls=%async_computation.23 | async-start | bytes 10485760 | tf_op jit(solution)/shard_map/reduce_scatter | solution.py:276
  1543.0 479.7 %all-reduce.16.cloned.1.call-start = ((), (), s32[]{:S(2)}) async-start(), calls=%async_computation.17 | async-start | bytes 8388608 | tf_op jit(solution)/shard_map/psum | solution.py:256
  1555.2 509.2 %all-reduce.18.cloned.1.call-start = ((), (), s32[]{:S(2)}) async-start(), calls=%async_computation.25 | async-start | bytes 16777216 | tf_op jit(solution)/shard_map/psum | solution.py:284
  (77 other events, 532.9 us)
Sparse Core Ops, SparseCore 0:
  9.8 37.8 all-gather.11
  49.6 35.1 all-gather.9
  86.7 35.1 all-gather.7
  123.6 35.0 all-gather.13
  166.0 290.8 all-reduce.9
  458.6 86.4 all-gather.15
  546.9 87.4 all-gather.17
  636.2 87.3 all-gather.19
  738.3 290.8 all-reduce.11
  1088.7 289.7 all-reduce.13
  1433.7 34.1 reduce-scatter.11
  1486.5 33.7 reduce-scatter.9
  1523.2 35.1 reduce-scatter.13
  1561.3 35.1 reduce-scatter.7
  1599.4 86.3 reduce-scatter.19
  1689.3 86.3 reduce-scatter.15
  1778.5 86.3 reduce-scatter.17
  1867.7 154.9 all-reduce.15
  2026.0 38.3 all-reduce.17
where the time goes:
time: 2090 us
  waiting for transfers between devices  1650 us (79%)
  matrix products  236 us (11%)
  other arithmetic  103 us (5%)
  blocking collectives  49.6 us (2%)
  local copies, waits for them, and re-layouts  34.5 us (2%)
    psum x1, waiting for transfers between devices, shards(): down_raw = lax.psum(plain_dot(mixed_act, full_down), 'col')  291 us
    psum x1, waiting for transfers between devices, shards(): attn_raw = lax.psum(plain_dot(attended_flat, full_out), 'col')  289 us
    psum x1, waiting for transfers between devices, shards(): grad_hidden = grad_y + lax.psum(mlp_part, 'col')  288 us
    psum x1, waiting for transfers between devices, shards(): lax.psum(input_part.astype(jnp.bfloat16), 'col').astype(jnp.float32)  129 us
    reduce_scatter x1, waiting for transfers between devices, shards(): lax.psum_scatter(grad_w_gate.astype(jnp.bfloat16), 'row', scatter_dimensi...  89.8 us
    reduce_scatter x1, waiting for transfers between devices, shards(): lax.psum_scatter(grad_w_down.astype(jnp.bfloat16), 'row', scatter_dimensi...  89.3 us
    reduce_scatter x1, waiting for transfers between devices, shards(): lax.psum_scatter(grad_w_up.astype(jnp.bfloat16), 'row', scatter_dimension...  89.3 us
    all_gather x1, waiting for transfers between devices, shards(): lax.all_gather(w_gate, 'row', axis=0, tiled=True)  77.5 us
  transfers between devices with their start and end apart: 19, of which 16 were waited for; matrix products, arithmetic and copies ran while one was open for 10% of the time, Pallas kernels for 0%

commit v1 on v0

--- a/solution.py
+++ b/solution.py
@@ -181,7 +181,9 @@
     seg_view = segment_ids.reshape(seq_count, LEN)
     attended, log_total = lax.map(attend_forward, (query_rot, key_rot, value_heads, seg_view))
     attended_flat = attended.reshape(tokens_here, local_width)
-    attn_raw = lax.psum(plain_dot(attended_flat, full_out), "col")
+    x = plain_dot(attended_flat, full_out)
+    terms = lax.all_gather(x, "col", axis=0, tiled=False)
+    attn_raw = terms.sum(axis=0)
     attn_scale = lax.rsqrt(jnp.mean(attn_raw * attn_raw, axis=1, keepdims=True) + EPS)
     attn_unit = attn_raw * attn_scale
     hidden = block_input.astype(jnp.float32) + attn_unit * attn_gain

time: 2090 us -> 2360 us (1.13)
  waiting for transfers between devices: 1650 us -> 1900 us
    all_gather x0 -> x1, waiting for transfers between devices: none -> 559 us  [shards(): terms = lax.all_gather(x, 'col', axis=0, tiled=False)]
    psum x1 -> x0, waiting for transfers between devices: 289 us -> none  [shards(): attn_raw = lax.psum(plain_dot(attended_flat, full_out), 'col')]
where the time goes in v1:
time: 2360 us
  waiting for transfers between devices  1900 us (81%)
  matrix products  237 us (10%)
  other arithmetic  119 us (5%)
  blocking collectives  49.6 us (2%)
  local copies, waits for them, and re-layouts  34.6 us (1%)
    all_gather x1, waiting for transfers between devices, shards(): terms = lax.all_gather(x, 'col', axis=0, tiled=False)  559 us
    psum x1, waiting for transfers between devices, shards(): down_raw = lax.psum(plain_dot(mixed_act, full_down), 'col')  291 us
    psum x1, waiting for transfers between devices, shards(): grad_hidden = grad_y + lax.psum(mlp_part, 'col')  288 us
    psum x1, waiting for transfers between devices, shards(): lax.psum(input_part.astype(jnp.bfloat16), 'col').astype(jnp.float32)  129 us
    reduce_scatter x1, waiting for transfers between devices, shards(): lax.psum_scatter(grad_w_gate.astype(jnp.bfloat16), 'row', scatter_dimensi...  89.8 us
    reduce_scatter x1, waiting for transfers between devices, shards(): lax.psum_scatter(grad_w_down.astype(jnp.bfloat16), 'row', scatter_dimensi...  89.3 us
    reduce_scatter x1, waiting for transfers between devices, shards(): lax.psum_scatter(grad_w_up.astype(jnp.bfloat16), 'row', scatter_dimension...  89.2 us
    all_gather x1, waiting for transfers between devices, shards(): lax.all_gather(w_up, 'row', axis=0, tiled=True)  74.8 us
  transfers between devices with their start and end apart: 19, of which 16 were waited for; matrix products, arithmetic and copies ran while one was open for 10% of the time, Pallas kernels for 0%

profile of v1, /device:TPU:0, one launch (start us, length us, event | category | flops | bytes accessed | tf_op | source)
XLA Modules:
  0.0 2355.3 jit_solution(7983721926833220822)
XLA Ops:
  15.1 32.7 %all-gather.14.cloned.1.call-done = bf16[2048,512]{1,0:T(8,128)(2,1)} async-done(((bf16[512,512]{1,0:T(8,128)(2,1)}), bf16[2048,512]{1,0:T(8,128)(2,1)}) %all-gather.14.cloned.1.call-update) | async-done | bytes 2097168 | tf_op jit(solution)/shard_map/all_gather | solution.py:149
  54.4 30.5 %all-gather.12.cloned.1.call-done = bf16[2048,512]{1,0:T(8,128)(2,1)} async-done(((bf16[512,512]{1,0:T(8,128)(2,1)}), bf16[2048,512]{1,0:T(8,128)(2,1)}) %all-gather.12.cloned.1.call-update) | async-done | bytes 2097168 | tf_op jit(solution)/shard_map/all_gather | solution.py:148
  141.4 17.3 all-gather.16.cloned.1.call-done
  168.1 559.4 %all-gather.24.cloned.1.call-done = f32[4096,2048]{1,0:T(8,128)} async-done(((f32[1024,2048]{1,0:T(8,128)}), f32[4096,2048]{1,0:T(8,128)}) %all-gather.24.cloned.1.call-update) | async-done | bytes 33554448 | tf_op jit(solution)/shard_map/all_gather | solution.py:185
  727.5 17.4 reduce_sum.151
  755.2 59.7 %all-gather.18.cloned.1.call-done = bf16[2048,2048]{1,0:T(8,128)(2,1)} async-done(((bf16[512,2048]{1,0:T(8,128)(2,1)}), bf16[2048,2048]{1,0:T(8,128)(2,1)}) %all-gather.18.cloned.1.call-update) | async-done | bytes 8388624 | tf_op jit(solution)/shard_map/all_gather | solution.py:152
  814.9 14.6 fusion.42
  829.4 74.8 %all-gather.20.cloned.1.call-done = bf16[2048,2048]{1,0:T(8,128)(2,1)} async-done(((bf16[512,2048]{1,0:T(8,128)(2,1)}), bf16[2048,2048]{1,0:T(8,128)(2,1)}) %all-gather.20.cloned.1.call-update) | async-done | bytes 8388624 | tf_op jit(solution)/shard_map/all_gather | solution.py:153
  904.2 17.0 multiply_convert_fusion.5
  921.2 72.2 %all-gather.22.cloned.1.call-done = bf16[2048,2048]{1,0:T(8,128)(2,1)} async-done(((bf16[2048,512]{1,0:T(8,128)(2,1)}), bf16[2048,2048]{1,0:T(8,128)(2,1)}) %all-gather.22.cloned.1.call-update) | async-done | bytes 8388624 | tf_op jit(solution)/shard_map/all_gather | solution.py:154
  993.4 14.5 fusion.43
  1008.2 290.7 %all-reduce.9.cloned.1.call-done = f32[1024,2048]{1,0:T(8,128)} async-done(((f32[1024,2048]{1,0:T(8,128)}), f32[1024,2048]{1,0:T(8,128)}) %all-reduce.9.cloned.1.call-update) | async-done | bytes 8388624 | tf_op jit(solution)/shard_map/psum | solution.py:196
  1312.1 19.8 multiply_convert_fusion.3
  1360.4 287.9 %all-reduce.11.cloned.1.call-done = f32[1024,2048]{1,0:T(8,128)} async-done(((f32[1024,2048]{1,0:T(8,128)}), f32[1024,2048]{1,0:T(8,128)}) %all-reduce.11.cloned.1.call-update) | async-done | bytes 8388624 | tf_op jit(solution)/shard_map/psum | solution.py:225
  1769.4 14.4 convolution_convert_fusion
  1783.9 14.1 convolution_convert_fusion.2
  1798.0 14.7 convolution_convert_fusion.1
  1828.2 38.0 %reduce-scatter.8.cloned.1.call-done = bf16[512,512]{0,1:T(8,128)(2,1)} async-done(((bf16[2048,512]{0,1:T(8,128)(2,1)}), bf16[512,512]{0,1:T(8,128)(2,1)}) %reduce-scatter.8.cloned.1.call-update) | async-done | bytes 524304 | tf_op jit(solution)/shard_map/reduce_scatter | solution.py:263
  1866.3 89.3 %reduce-scatter.20.cloned.1.call-done = bf16[2048,512]{1,0:T(8,128)(2,1)} async-done(((bf16[2048,2048]{1,0:T(8,128)(2,1)}), bf16[2048,512]{1,0:T(8,128)(2,1)}) %reduce-scatter.20.cloned.1.call-update) | async-done | bytes 2097168 | tf_op jit(solution)/shard_map/reduce_scatter | solution.py:281
  1955.5 89.8 %reduce-scatter.16.cloned.1.call-done = bf16[512,2048]{1,0:T(8,128)(2,1)} async-done(((bf16[2048,2048]{1,0:T(8,128)(2,1)}), bf16[512,2048]{1,0:T(8,128)(2,1)}) %reduce-scatter.16.cloned.1.call-update) | async-done | bytes 2097168 | tf_op jit(solution)/shard_map/reduce_scatter | solution.py:275
  2045.4 89.2 %reduce-scatter.18.cloned.1.call-done = bf16[512,2048]{1,0:T(8,128)(2,1)} async-done(((bf16[2048,2048]{1,0:T(8,128)(2,1)}), bf16[512,2048]{1,0:T(8,128)(2,1)}) %reduce-scatter.18.cloned.1.call-update) | async-done | bytes 2097168 | tf_op jit(solution)/shard_map/reduce_scatter | solution.py:278
  2135.3 27.9 %all-reduce = (f32[512]{0:T(512)}, f32[512]{0:T(512)}, f32[2048]{0:T(1024)}, f32[2048]{0:T(1024)}) all-reduce(f32[512]{0:T(512)S(1)} %get-tuple-element.86, f32[512]{0:T(512)S(1)} %get-tuple-element.84, f32[2048]{0:T(1024)S(1)} %copy-done.64, f32[2048]{0:T(1024)S(1)} %copy-done.65), channel_id=1, replica_groups=mesh['dp'=2,'row'=4,'col'=4] {'dp','row'}, use_global_device_ids=true, to_apply=%region_36.37 | all-reduce | flops 5120 | bytes 40960 | tf_op jit(solution)/shard_map/psum | solution.py:294
  2163.2 129.2 %all-reduce.13.cloned.1.call-done = bf16[1024,2048]{1,0:T(8,128)(2,1)} async-done(((bf16[1024,2048]{1,0:T(8,128)(2,1)}), bf16[1024,2048]{1,0:T(8,128)(2,1)}) %all-reduce.13.cloned.1.call-update) | async-done | bytes 4194320 | tf_op jit(solution)/shard_map/psum | solution.py:258
  2304.5 29.7 %all-reduce.15.cloned.1.call-done = (bf16[512,512]{0,1:T(8,128)(2,1)}, bf16[512,512]{0,1:T(8,128)(2,1)}, bf16[512,512]{0,1:T(8,128)(2,1)}, bf16[512,512]{1,0:T(8...) async-done(((bf16[512,512]{0,1:T(8,128)(2,1)}, bf16[512,512]{0,1:T(8,128)(2,1)}, bf16[512,512]{0,1:T(8,128)(2,1)}, ...) | async-done | bytes 8388624 | tf_op jit(solution)/shard_map/psum | solution.py:286
  (292 shorter events, 295.0 us)
Async XLA Ops:
  7.2 40.6 %all-gather.14.cloned.1.call-start = ((), (), s32[]{:S(2)}) async-start(), calls=%async_computation.9 | async-start | bytes 2621440 | tf_op jit(solution)/shard_map/all_gather | solution.py:149
  7.9 76.9 %all-gather.12.cloned.1.call-start = ((), (), s32[]{:S(2)}) async-start(), calls=%async_computation.8 | async-start | bytes 2621440 | tf_op jit(solution)/shard_map/all_gather | solution.py:148
  8.7 119.8 %all-gather.10.cloned.1.call-start = ((), (), s32[]{:S(2)}) async-start(), calls=%async_computation.7 | async-start | bytes 2621440 | tf_op jit(solution)/shard_map/all_gather | solution.py:150
  9.4 149.2 %all-gather.16.cloned.1.call-start = ((), (), s32[]{:S(2)}) async-start(), calls=%async_computation.10 | async-start | bytes 2621440 | tf_op jit(solution)/shard_map/all_gather | solution.py:151
  10.0 717.5 %all-gather.24.cloned.1.call-start = ((), (), s32[]{:S(2)}) async-start(), calls=%async_computation.24 | async-start | bytes 41943040 | tf_op jit(solution)/shard_map/all_gather | solution.py:185
  12.8 103.1 %copy-start.22 = (f32[1024,128]{1,0:T(8,128)}, f32[1024,128]{1,0:T(8,128)S(1)}, u32[]{:S(2)}) copy-start(f32[1024,128]{1,0:T(8,128)S(1)} %pad_maximum_fusion.2) | copy-start | bytes 1572868
  13.1 102.9 %copy-start.27 = (f32[1024,128]{1,0:T(8,128)}, f32[1024,128]{1,0:T(8,128)S(1)}, u32[]{:S(2)}) copy-start(f32[1024,128]{1,0:T(8,128)S(1)} %pad_maximum_fusion.3) | copy-start | bytes 1572868
  165.9 648.9 %all-gather.18.cloned.1.call-start = ((), (), s32[]{:S(2)}) async-start(), calls=%async_computation.11 | async-start | bytes 10485760 | tf_op jit(solution)/shard_map/all_gather | solution.py:152
  166.5 737.7 %all-gather.20.cloned.1.call-start = ((), (), s32[]{:S(2)}) async-start(), calls=%async_computation.12 | async-start | bytes 10485760 | tf_op jit(solution)/shard_map/all_gather | solution.py:153
  167.3 826.2 %all-gather.22.cloned.1.call-start = ((), (), s32[]{:S(2)}) async-start(), calls=%async_computation.13 | async-start | bytes 10485760 | tf_op jit(solution)/shard_map/all_gather | solution.py:154
  168.0 1130.9 %all-reduce.9.cloned.1.call-start = ((), (), s32[]{:S(2)}) async-start(), calls=%async_computation.14 | async-start | bytes 16777216 | tf_op jit(solution)/shard_map/psum | solution.py:196
  1008.0 295.1 %copy-start.55 = (f32[2048]{0:T(1024)S(1)}, f32[2048]{0:T(1024)}, u32[]{:S(2)}) copy-start(f32[2048]{0:T(1024)} %param.28) | copy-start | bytes 24580
  1008.0 640.3 %all-reduce.11.cloned.1.call-start = ((), (), s32[]{:S(2)}) async-start(), calls=%async_computation.15 | async-start | bytes 16777216 | tf_op jit(solution)/shard_map/psum | solution.py:225
  1358.3 290.0 %copy-start.57 = (f32[2048]{0:T(1024)S(1)}, f32[2048]{0:T(1024)}, u32[]{:S(2)}) copy-start(f32[2048]{0:T(1024)} %param.27) | copy-start | bytes 24580
  1358.3 290.0 %copy-start.63 = (f32[1024]{0:T(1024)S(1)}, f32[1024]{0:T(1024)}, u32[]{:S(2)}) copy-start(f32[1024]{0:T(1024)} %copy-done.62) | copy-start | bytes 12292
  1358.3 466.7 %reduce-scatter.12.cloned.1.call-start = ((), (), s32[]{:S(2)}) async-start(), calls=%async_computation.19 | async-start | bytes 2621440 | tf_op jit(solution)/shard_map/reduce_scatter | solution.py:269
  1703.3 121.7 %reduce-scatter.10.cloned.1.call-start = ((), (), s32[]{:S(2)}) async-start(), calls=%async_computation.18 | async-start | bytes 2621440 | tf_op jit(solution)/shard_map/reduce_scatter | solution.py:266
  1756.2 72.1 %reduce-scatter.14.cloned.1.call-start = ((), (), s32[]{:S(2)}) async-start(), calls=%async_computation.20 | async-start | bytes 2621440 | tf_op jit(solution)/shard_map/reduce_scatter | solution.py:272
  1762.4 103.8 %reduce-scatter.8.cloned.1.call-start = ((), (), s32[]{:S(2)}) async-start(), calls=%async_computation.17 | async-start | bytes 2621440 | tf_op jit(solution)/shard_map/reduce_scatter | solution.py:263
  1769.3 186.2 %reduce-scatter.20.cloned.1.call-start = ((), (), s32[]{:S(2)}) async-start(), calls=%async_computation.23 | async-start | bytes 10485760 | tf_op jit(solution)/shard_map/reduce_scatter | solution.py:281
  1783.9 261.5 %reduce-scatter.16.cloned.1.call-start = ((), (), s32[]{:S(2)}) async-start(), calls=%async_computation.21 | async-start | bytes 10485760 | tf_op jit(solution)/shard_map/reduce_scatter | solution.py:275
  1798.0 336.6 %reduce-scatter.18.cloned.1.call-start = ((), (), s32[]{:S(2)}) async-start(), calls=%async_computation.22 | async-start | bytes 10485760 | tf_op jit(solution)/shard_map/reduce_scatter | solution.py:278
  1812.8 479.7 %all-reduce.13.cloned.1.call-start = ((), (), s32[]{:S(2)}) async-start(), calls=%async_computation.16 | async-start | bytes 8388608 | tf_op jit(solution)/shard_map/psum | solution.py:258
  1825.0 509.2 %all-reduce.15.cloned.1.call-start = ((), (), s32[]{:S(2)}) async-start(), calls=%async_computation.25 | async-start | bytes 16777216 | tf_op jit(solution)/shard_map/psum | solution.py:286
  (77 other events, 436.1 us)
Sparse Core Ops, SparseCore 0:
  9.8 37.8 all-gather.13
  49.6 35.1 all-gather.11
  86.7 35.1 all-gather.9
  123.6 35.0 all-gather.15
  166.1 561.3 all-gather.23
  729.2 85.6 all-gather.17
  816.7 87.4 all-gather.19
  906.1 87.3 all-gather.21
  1008.1 290.8 all-reduce.8
  1358.4 289.7 all-reduce.10
  1703.4 34.1 reduce-scatter.11
  1756.3 33.7 reduce-scatter.9
  1793.0 35.1 reduce-scatter.13
  1831.0 35.1 reduce-scatter.7
  1869.2 86.3 reduce-scatter.19
  1959.0 86.3 reduce-scatter.15
  2048.3 86.2 reduce-scatter.17
  2137.4 154.9 all-reduce.12
  2295.8 38.3 all-reduce.14
